TPU v7x, 32 devices: a whole 2x2x4 slice. The times are simulated.
32 devices in a mesh: dp: 8 (over z, core), resp: 4 (over y, x).
Axes of the slice: x: 2, y: 2, z: 4, core: 2. Of those that a mesh axis runs over, the one named last changes fastest.
Arguments:
- queries: bfloat16 [8, 4, 128, 4096], P('dp', 'resp'), may hold values from -6 to 6
- prefix_kv: bfloat16 [8, 256, 1024], P('dp', 'resp'), may hold values from -6 to 6
- resp_kv: bfloat16 [8, 4, 128, 1024], P('dp', 'resp'), may hold values from -6 to 6
- direction: bfloat16 [8, 4, 128, 4096], P('dp', 'resp'), may hold values from -0.09375 to 0.09375
- base_logprob: float32 [8, 4, 128], P('dp', 'resp'), may hold values from -2 to 2
- rollout_logprob: float32 [8, 4, 128], P('dp', 'resp'), may hold values from -2 to 2
- destination: int32 [8, 4, 128], P('dp', 'resp'), may hold values from 0 to 1023, as said below
- advantage: float32 [8, 4], P('dp', 'resp'), may hold values from -4 to 4
- lengths: int32 [8, 4], P('dp', 'resp'), may hold values from 1 to 128, 384 in all within a row
- prefix_blocks: int32 [8, 4], P('dp', 'resp'), may hold values from 1 to 2, as said below
Outputs:
- query_grad: bfloat16 [8, 4, 128, 4096], P('dp', 'resp')
- resp_grad: bfloat16 [8, 4, 128, 1024], P('dp', 'resp')
- prefix_grad: bfloat16 [8, 256, 1024], P('dp', 'resp')
Inputs may be any that keep to these rules, and one draw needn't show every extreme that they name: For each response index r, destination maps the 1024 rollout rows one to one onto the trainer rows; value g * 128 + t names token t of prompt group g; every index of dp holds exactly 16 rows bound for each prompt group. Each response sees the leading prefix_blocks blocks of 128 prompt rows; in every prompt group some response sees all 2. In every prompt group the lengths sum to 384 and one response has 128.
All inputs are finite; a program needn't handle non-finite values.
Results may differ from a plain program's by a relative error of at most 0.011.
Values may be sent and summed in bfloat16 or wider, within the bound.
A program may use at most 128 MiB of HBM per device.

v0:
```python
import math
import jax
import jax.numpy as jnp
from jax import lax
from jax.sharding import PartitionSpec as P

QH = 32
KVH = 4
HD = 128
GQ = 8
BLOCK = 128
loss_scale = 65536.0
clip_lower = 0.8
clip_upper = 1.28


def split_heads(keys_values):
    total_keys = keys_values.shape[0]
    key_heads = keys_values[:, : KVH * HD].reshape(total_keys, KVH, HD).transpose(1, 0, 2)
    value_heads = keys_values[:, KVH * HD :].reshape(total_keys, KVH, HD).transpose(1, 0, 2)
    return (key_heads, value_heads)


def body(
    queries,
    prefix_kv,
    resp_kv,
    direction,
    base_logprob,
    rollout_logprob,
    destination,
    advantage,
    lengths,
    prefix_blocks,
):
    tok_rows = queries.shape[2]
    score_scale = 1.0 / math.sqrt(HD)
    dp_count = lax.axis_size("dp")
    per_peer = tok_rows // dp_count
    targets = destination[0, 0] // tok_rows
    ordering = jnp.argsort(targets, stable=True)
    sent_logprob = rollout_logprob[0, 0][ordering].reshape(dp_count, per_peer)
    sent_slot = (destination[0, 0] % tok_rows)[ordering].reshape(dp_count, per_peer)
    got_logprob, got_slot = (
        lax.all_to_all(sent_logprob, "dp", split_axis=0, concat_axis=0, tiled=True),
        lax.all_to_all(sent_slot, "dp", split_axis=0, concat_axis=0, tiled=True),
    )
    old_rows = (
        jnp.zeros((tok_rows,), jnp.float32).at[got_slot.reshape(-1)].set(got_logprob.reshape(-1))
    )
    prefix_all = lax.all_gather(prefix_kv[0], "resp", axis=0, tiled=True)
    prefix_rows = prefix_all.shape[0]
    total_keys = prefix_rows + tok_rows
    own_kv = resp_kv[0, 0]
    key_heads, value_heads = split_heads(jnp.concatenate([prefix_all, own_kv], axis=0))
    key_index = jnp.arange(total_keys, dtype=jnp.int32)
    query_index = jnp.arange(tok_rows, dtype=jnp.int32)
    in_prefix = (key_index < prefix_rows) & (key_index // BLOCK < prefix_blocks[0, 0])
    in_response = (key_index[None, :] >= prefix_rows) & (
        key_index[None, :] - prefix_rows <= query_index[:, None]
    )
    allowed = in_prefix[None, :] | in_response
    query_heads = queries[0, 0].reshape(tok_rows, KVH, GQ, HD).transpose(1, 0, 2, 3)

    def head_forward(head_inputs):
        query_head, key_head, value_head = head_inputs
        scores = (
            jnp.einsum("rgd,ld->grl", query_head, key_head, preferred_element_type=jnp.float32)
            * score_scale
        )
        scores = jnp.where(allowed[None], scores, -1e30)
        shifted = jnp.exp(scores - jnp.max(scores, axis=-1, keepdims=True))
        prob_bf16 = (shifted / jnp.sum(shifted, axis=-1, keepdims=True)).astype(jnp.bfloat16)
        head_out = jnp.einsum(
            "grl,ld->rgd", prob_bf16, value_head, preferred_element_type=jnp.float32
        )
        return (prob_bf16, head_out)

    prob_all, out_all = lax.map(head_forward, (query_heads, key_heads, value_heads))
    attn_out = out_all.transpose(1, 0, 2, 3).reshape(tok_rows, QH * HD)
    out_bf16 = attn_out.astype(jnp.bfloat16)
    direction_rows = direction[0, 0]
    new_logprob = base_logprob[0, 0] + jnp.einsum(
        "rj,rj->r", out_bf16, direction_rows, preferred_element_type=jnp.float32
    )
    ratio_weight = jnp.clip(jnp.exp(new_logprob - old_rows), clip_lower, clip_upper)
    length_one = lengths[0, 0]
    loss_coeff = jnp.where(
        query_index < length_one,
        -loss_scale * ratio_weight * advantage[0, 0] / length_one.astype(jnp.float32),
        0.0,
    )
    grad_out = (loss_coeff[:, None] * direction_rows.astype(jnp.float32)).astype(jnp.bfloat16)
    grad_heads = grad_out.reshape(tok_rows, KVH, GQ, HD).transpose(1, 0, 2, 3)

    def head_backward(head_inputs):
        key_head, value_head, prob_bf16, head_out, grad_head = head_inputs
        prob_grad = jnp.einsum(
            "rgd,ld->grl", grad_head, value_head, preferred_element_type=jnp.float32
        )
        row_delta = jnp.sum(grad_head.astype(jnp.float32) * head_out, axis=-1).T
        dscore = (
            prob_bf16.astype(jnp.float32) * (prob_grad - row_delta[..., None]) * score_scale
        ).astype(jnp.bfloat16)
        query_part = jnp.einsum("grl,ld->rgd", dscore, key_head, preferred_element_type=jnp.float32)
        return (query_part, dscore)

    query_parts, dscore_all = lax.map(
        head_backward, (key_heads, value_heads, prob_all, out_all, grad_heads)
    )
    query_grad = query_parts.transpose(1, 0, 2, 3).reshape(tok_rows, QH * HD).astype(jnp.bfloat16)
    key_part = jnp.einsum(
        "hgrl,hrgd->lhd", dscore_all, query_heads, preferred_element_type=jnp.float32
    )
    value_part = jnp.einsum(
        "hgrl,hrgd->lhd", prob_all, grad_heads, preferred_element_type=jnp.float32
    )
    kv_grad = jnp.concatenate(
        [key_part.reshape(total_keys, KVH * HD), value_part.reshape(total_keys, KVH * HD)], axis=1
    )
    summed = lax.psum_scatter(kv_grad[:prefix_rows], "resp", scatter_dimension=0, tiled=True)
    resp_part = kv_grad[prefix_rows:]
    return (
        query_grad[None, None],
        resp_part.astype(jnp.bfloat16)[None, None],
        summed.astype(jnp.bfloat16)[None],
    )


def solution(mesh):
    return jax.shard_map(
        body,
        mesh=mesh,
        in_specs=(
            P("dp", "resp", None, None),
            P("dp", "resp", None),
            P("dp", "resp", None, None),
            P("dp", "resp", None, None),
            P("dp", "resp", None),
            P("dp", "resp", None),
            P("dp", "resp", None),
            P("dp", "resp"),
            P("dp", "resp"),
            P("dp", "resp"),
        ),
        out_specs=(P("dp", "resp", None, None), P("dp", "resp", None, None), P("dp", "resp", None)),
        check_vma=False,
    )
```

profile of v0, /device:TPU:0, one launch (start us, length us, event | category | flops | bytes accessed | tf_op | source)
XLA Modules:
  0.0 153.7 jit_solution(10298874838395375511)
XLA Ops:
  8.0 2.5 %sort.17 = (s32[128]{0:T(128)}, s32[128]{0:T(128)S(1)}) sort(s32[128]{0:T(128)S(1)} %get-tuple-element.195, s32[128]{0:T(128)S(1)} %iota.29), dimensions={0}, to_apply=%region_4.5 | sort | flops 896 | bytes 2048 | tf_op jit(solution)/shard_map/jit(argsort)/sort | solution.py:41
  10.5 1.2 gather_fusion
  12.4 6.3 %all-to-all-start = ((s32[8,1,16]{2,1,0:T(1,128)}), s32[8,1,16]{2,1,0:T(1,128)S(1)}, u32[]{:S(2)}, u32[]{:S(2)}) async-start(s32[8,1,16]{2,1,0:T(1,128)} %bitcast.29), calls=%async_computation | async-start | bytes 8192 | tf_op jit(solution)/shard_map/all_to_all | solution.py:46
  18.8 11.5 %all-gather = bf16[1,256,1024]{2,1,0:T(8,128)(2,1)S(1)} all-gather(bf16[1,64,1024]{2,1,0:T(8,128)(2,1)} %param.15), channel_id=2, replica_groups=mesh['dp'=8,'resp'=4] {'resp'}, dimensions={1}, use_global_device_ids=true | all-gather | bytes 655360 | tf_op jit(solution)/shard_map/all_gather | solution.py:51
  32.9 2.4 %broadcast.103.clone = bf16[4,8,128,384]{2,3,1,0:T(8,128)(2,1)} broadcast(bf16[]{:T(256)} %constant.89.clone.1), dimensions={} | broadcast | bytes 3145730 | tf_op jit(solution)/shard_map/broadcast.12
  35.3 15.7 %while.28 = (s32[]{:T(128)}, bf16[4,8,128,384]{2,3,1,0:T(8,128)(2,1)}, f32[4,128,8,128]{1,3,2,0:T(8,128)}, bf16[4,384,128]{1,2,0:T(8,128)(2,1)S(1)}, bf16[4,128,...) while((s32[]{:T(128)}, ...), condition=%wide.region_3.4_spmd.clone.clone, body=%wide.region_0.0_spmd.clone.sunk.clone | while | flops 306464512 | bytes 5444501 | solution.py:79
  37.5 1.7 %fusion.113 = f32[4,128,8,128]{1,3,2,0:T(8,128)} fusion(f32[4,128,8,128]{1,3,2,0:T(8,128)} %get-tuple-element.364, s32[]{:T(128)} %get-tuple-element.362, bf16[4,384,128]{1,2,0:T(8,128)(2,1)S(1)} %get-tuple-element.376, f32[8,128]{1,0:T(8,128)S(1)} %get-tuple-element.342, pred[128,384]{0,1:T(8,128)(4,1)S(1)} %fusion.111, ...), kind=kOutput, calls=%fused_computation.28.clone.1.clone | convolution fusion | flops 203294080 | bytes 1038336 | tf_op jit(solution)/shard_map/while/body/eval_jaxpr/grl,ld->rgd/dot_general | solution.py:74
  41.4 1.8 %fusion.113 = f32[4,128,8,128]{1,3,2,0:T(8,128)} fusion(f32[4,128,8,128]{1,3,2,0:T(8,128)} %get-tuple-element.364, s32[]{:T(128)} %get-tuple-element.362, bf16[4,384,128]{1,2,0:T(8,128)(2,1)S(1)} %get-tuple-element.376, f32[8,128]{1,0:T(8,128)S(1)} %get-tuple-element.342, pred[128,384]{0,1:T(8,128)(4,1)S(1)} %fusion.111, ...), kind=kOutput, calls=%fused_computation.28.clone.1.clone | convolution fusion | flops 203294080 | bytes 1038336 | tf_op jit(solution)/shard_map/while/body/eval_jaxpr/grl,ld->rgd/dot_general | solution.py:74
  45.3 1.7 %fusion.113 = f32[4,128,8,128]{1,3,2,0:T(8,128)} fusion(f32[4,128,8,128]{1,3,2,0:T(8,128)} %get-tuple-element.364, s32[]{:T(128)} %get-tuple-element.362, bf16[4,384,128]{1,2,0:T(8,128)(2,1)S(1)} %get-tuple-element.376, f32[8,128]{1,0:T(8,128)S(1)} %get-tuple-element.342, pred[128,384]{0,1:T(8,128)(4,1)S(1)} %fusion.111, ...), kind=kOutput, calls=%fused_computation.28.clone.1.clone | convolution fusion | flops 203294080 | bytes 1038336 | tf_op jit(solution)/shard_map/while/body/eval_jaxpr/grl,ld->rgd/dot_general | solution.py:74
  49.3 1.7 %fusion.113 = f32[4,128,8,128]{1,3,2,0:T(8,128)} fusion(f32[4,128,8,128]{1,3,2,0:T(8,128)} %get-tuple-element.364, s32[]{:T(128)} %get-tuple-element.362, bf16[4,384,128]{1,2,0:T(8,128)(2,1)S(1)} %get-tuple-element.376, f32[8,128]{1,0:T(8,128)S(1)} %get-tuple-element.342, pred[128,384]{0,1:T(8,128)(4,1)S(1)} %fusion.111, ...), kind=kOutput, calls=%fused_computation.28.clone.1.clone | convolution fusion | flops 203294080 | bytes 1038336 | tf_op jit(solution)/shard_map/while/body/eval_jaxpr/grl,ld->rgd/dot_general | solution.py:74
  52.1 3.1 %bitcast_convert_fusion = f32[128,4096]{0,1:T(8,128)} fusion(f32[4,128,8,128]{1,3,2,0:T(8,128)} %get-tuple-element.387), kind=kLoop, calls=%fused_computation.54 | loop fusion | flops 1048576 | bytes 4194304
  55.2 2.0 %copy.65 = f32[128,4096]{1,0:T(8,128)S(1)} copy(f32[128,4096]{0,1:T(8,128)} %bitcast_convert_fusion) | data formatting | bytes 4194304
  59.3 2.4 %copy.51 = bf16[1,1,128,4096]{2,3,1,0:T(8,128)(2,1)} copy(bf16[1,1,128,4096]{3,2,1,0:T(8,128)(2,1)} %param.17) | data formatting | bytes 2097152 | tf_op args[3]
  61.7 1.3 gather_fusion.1
  65.1 4.5 %all-to-all-start.1 = ((f32[8,1,16]{2,1,0:T(1,128)}), f32[8,1,16]{2,1,0:T(1,128)S(1)}, u32[]{:S(2)}, u32[]{:S(2)}) async-start(f32[8,1,16]{2,1,0:T(1,128)} %bitcast.32), calls=%async_computation.1 | async-start | bytes 8192 | tf_op jit(solution)/shard_map/all_to_all | solution.py:45
  71.4 3.7 %all-to-all-done.1 = f32[8,1,16]{2,1,0:T(1,128)S(1)} async-done(((f32[8,1,16]{2,1,0:T(1,128)}), f32[8,1,16]{2,1,0:T(1,128)S(1)}, u32[]{:S(2)}, u32[]{:S(2)}) %all-to-all-start.1) | async-done | bytes 544 | tf_op jit(solution)/shard_map/all_to_all | solution.py:45
  78.1 1.5 fusion.51
  79.6 1.9 %fusion.72 = f32[4,128,384,1]{2,1,3,0:T(8,128)} fusion(bf16[4,128,8,128]{1,3,2,0:T(8,128)(2,1)S(1)} %fusion.51, bf16[4,8,128,384]{2,3,1,0:T(8,128)(2,1)S(1)} %copy-done.1), kind=kOutput, calls=%fused_computation.94 | convolution fusion | flops 402653184 | bytes 4980736 | tf_op jit(solution)/shard_map/hgrl,hrgd->lhd/dot_general | solution.py:115
  81.5 2.4 %broadcast.103 = bf16[4,8,128,384]{2,3,1,0:T(8,128)(2,1)} broadcast(bf16[]{:T(256)} %constant.89.clone.1), dimensions={} | broadcast | bytes 3145730 | tf_op jit(solution)/shard_map/broadcast.12
  83.9 30.5 %while.27 = (s32[]{:T(128)}, bf16[4,128,8,128]{1,3,2,0:T(8,128)(2,1)}, bf16[4,8,128,384]{2,3,1,0:T(8,128)(2,1)}, bf16[4,384,128]{1,2,0:T(8,128)(2,1)}, bf16[4,8,...) while((s32[]{:T(128)}, ...), condition=%wide.region_8.9_spmd.clone, body=%wide.region_6.8_spmd.sunk.clone | while | flops 203684864 | bytes 29043384 | solution.py:108
  86.6 2.7 %bitcast_dynamic-update-slice_fusion.6 = (bf16[4,8,128,384]{2,3,1,0:T(8,128)(2,1)}, bf16[8,128,384]{1,2,0:T(8,128)(2,1)S(1)}) fusion(bf16[4,8,128,384]{2,3,1,0:T(8,128)(2,1)} %get-tuple-element.390, s32[]{:T(128)} %get-tuple-element.388, f32[8,128]{1,0:T(8,128)S(1)} %bitcast.236, bf16[4,128,8,128]{1,3,2,0:T(8,128)(2,1)} %get-tuple-element.402, ...), kind=kOutput, calls=%fused_computation.10.clone.1.clone | convolution fusion | flops 102629376 | bytes 2725376 | tf_op jit(solution)/shard_map/while/body/eval_jaxpr/rgd,ld->grl/dot_general | solution.py:98
  89.3 1.2 fusion.105
  94.2 2.7 %bitcast_dynamic-update-slice_fusion.6 = (bf16[4,8,128,384]{2,3,1,0:T(8,128)(2,1)}, bf16[8,128,384]{1,2,0:T(8,128)(2,1)S(1)}) fusion(bf16[4,8,128,384]{2,3,1,0:T(8,128)(2,1)} %get-tuple-element.390, s32[]{:T(128)} %get-tuple-element.388, f32[8,128]{1,0:T(8,128)S(1)} %bitcast.236, bf16[4,128,8,128]{1,3,2,0:T(8,128)(2,1)} %get-tuple-element.402, ...), kind=kOutput, calls=%fused_computation.10.clone.1.clone | convolution fusion | flops 102629376 | bytes 2725376 | tf_op jit(solution)/shard_map/while/body/eval_jaxpr/rgd,ld->grl/dot_general | solution.py:98
  97.0 1.2 fusion.105
  101.9 2.7 %bitcast_dynamic-update-slice_fusion.6 = (bf16[4,8,128,384]{2,3,1,0:T(8,128)(2,1)}, bf16[8,128,384]{1,2,0:T(8,128)(2,1)S(1)}) fusion(bf16[4,8,128,384]{2,3,1,0:T(8,128)(2,1)} %get-tuple-element.390, s32[]{:T(128)} %get-tuple-element.388, f32[8,128]{1,0:T(8,128)S(1)} %bitcast.236, bf16[4,128,8,128]{1,3,2,0:T(8,128)(2,1)} %get-tuple-element.402, ...), kind=kOutput, calls=%fused_computation.10.clone.1.clone | convolution fusion | flops 102629376 | bytes 2725376 | tf_op jit(solution)/shard_map/while/body/eval_jaxpr/rgd,ld->grl/dot_general | solution.py:98
  104.6 1.2 fusion.105
  109.5 2.7 %bitcast_dynamic-update-slice_fusion.6 = (bf16[4,8,128,384]{2,3,1,0:T(8,128)(2,1)}, bf16[8,128,384]{1,2,0:T(8,128)(2,1)S(1)}) fusion(bf16[4,8,128,384]{2,3,1,0:T(8,128)(2,1)} %get-tuple-element.390, s32[]{:T(128)} %get-tuple-element.388, f32[8,128]{1,0:T(8,128)S(1)} %bitcast.236, bf16[4,128,8,128]{1,3,2,0:T(8,128)(2,1)} %get-tuple-element.402, ...), kind=kOutput, calls=%fused_computation.10.clone.1.clone | convolution fusion | flops 102629376 | bytes 2725376 | tf_op jit(solution)/shard_map/while/body/eval_jaxpr/rgd,ld->grl/dot_general | solution.py:98
  112.2 1.2 fusion.105
  114.4 3.2 %fusion.71 = f32[4,384,128,1]{1,2,3,0:T(8,128)S(1)} fusion(bf16[4,8,128,384]{2,3,1,0:T(8,128)(2,1)} %get-tuple-element.407, bf16[4,128,8,128]{1,3,2,0:T(8,128)(2,1)} %copy-done.4), kind=kOutput, calls=%fused_computation.93 | convolution fusion | flops 402653184 | bytes 4980736 | tf_op jit(solution)/shard_map/hgrl,hrgd->lhd/dot_general | solution.py:112
  120.6 1.3 copy.70
  122.7 22.6 %reduce-scatter.2.cloned.1.call-done = f32[64,1024]{1,0:T(8,128)} async-done(((f32[256,1024]{1,0:T(8,128)}), f32[64,1024]{1,0:T(8,128)}) %reduce-scatter.2.cloned.1.call-update) | async-done | bytes 262160 | tf_op jit(solution)/shard_map/reduce_scatter | solution.py:121
  145.3 1.6 %convert_bitcast_fusion = bf16[1,64,1024]{2,1,0:T(8,128)(2,1)} fusion(f32[64,1024]{1,0:T(8,128)} %reduce-scatter.2.cloned.1.call-done), kind=kLoop, calls=%fused_computation.62 | loop fusion | flops 65536 | bytes 393216 | tf_op jit(solution)/shard_map/broadcast_in_dim | solution.py:126
  (125 shorter events, 38.9 us)
Async XLA Ops:
  7.2 54.6 %copy-start = (f32[1,1,128]{2,1,0:T(1,128)S(1)}, f32[1,1,128]{2,1,0:T(1,128)}, u32[]{:S(2)}) copy-start(f32[1,1,128]{2,1,0:T(1,128)} %param.19) | copy-start | bytes 1540
  7.2 23.4 %copy-start.12 = (bf16[1,1,128,1024]{3,2,1,0:T(8,128)(2,1)S(1)}, bf16[1,1,128,1024]{3,2,1,0:T(8,128)(2,1)}, u32[]{:S(2)}) copy-start(bf16[1,1,128,1024]{3,2,1,0:T(8,128)(2,1)} %param.16) | copy-start | bytes 786436
  7.2 23.5 %copy-start.11 = (bf16[1,1,128,4096]{3,2,1,0:T(8,128)(2,1)S(1)}, bf16[1,1,128,4096]{3,2,1,0:T(8,128)(2,1)}, u32[]{:S(2)}) copy-start(bf16[1,1,128,4096]{3,2,1,0:T(8,128)(2,1)} %param.14) | copy-start | bytes 3145732
  10.5 8.2 %copy-start.15 = (s32[1024]{0:T(1024)}, s32[1024]{0:T(1024)S(1)}, u32[]{:S(2)}) copy-start(s32[1024]{0:T(1024)S(1)} %pad_clamp_fusion) | copy-start | bytes 12292
  12.4 52.6 %all-to-all-start = ((s32[8,1,16]{2,1,0:T(1,128)}), s32[8,1,16]{2,1,0:T(1,128)S(1)}, u32[]{:S(2)}, u32[]{:S(2)}) async-start(s32[8,1,16]{2,1,0:T(1,128)} %bitcast.29), calls=%async_computation | async-start | bytes 8192 | tf_op jit(solution)/shard_map/all_to_all | solution.py:46
  32.9 2.4 %copy-start.10 = (bf16[384,512]{0,1:T(8,128)(2,1)S(1)}, bf16[384,512]{0,1:T(8,128)(2,1)}, u32[]{:S(2)}) copy-start(bf16[384,512]{0,1:T(8,128)(2,1)} %get-tuple-element.194) | copy-start | bytes 1179652
  35.3 0.5 copy-start.13
  37.5 1.7 %copy-start.14 = (pred[384]{0:T(512)(128)(4,1)S(1)}, pred[384]{0:T(512)(128)(4,1)}, u32[]{:S(2)}) copy-start(pred[384]{0:T(512)(128)(4,1)} %copy-done.13) | copy-start | bytes 1156 | tf_op jit(solution)/shard_map/while
  41.4 1.8 %copy-start.14 = (pred[384]{0:T(512)(128)(4,1)S(1)}, pred[384]{0:T(512)(128)(4,1)}, u32[]{:S(2)}) copy-start(pred[384]{0:T(512)(128)(4,1)} %copy-done.13) | copy-start | bytes 1156 | tf_op jit(solution)/shard_map/while
  43.2 0.5 copy-start.13
  45.3 1.7 %copy-start.14 = (pred[384]{0:T(512)(128)(4,1)S(1)}, pred[384]{0:T(512)(128)(4,1)}, u32[]{:S(2)}) copy-start(pred[384]{0:T(512)(128)(4,1)} %copy-done.13) | copy-start | bytes 1156 | tf_op jit(solution)/shard_map/while
  49.3 1.8 %copy-start.14 = (pred[384]{0:T(512)(128)(4,1)S(1)}, pred[384]{0:T(512)(128)(4,1)}, u32[]{:S(2)}) copy-start(pred[384]{0:T(512)(128)(4,1)} %copy-done.13) | copy-start | bytes 1156 | tf_op jit(solution)/shard_map/while
  51.0 1.1 copy-start.4
  55.2 2.0 %copy-start.5 = (bf16[1,1,128,4096]{3,2,1,0:T(8,128)(2,1)S(1)}, bf16[1,1,128,4096]{3,2,1,0:T(8,128)(2,1)}, u32[]{:S(2)}) copy-start(bf16[1,1,128,4096]{3,2,1,0:T(8,128)(2,1)} %param.17) | copy-start | bytes 3145732
  59.3 20.3 %copy-start.1 = (bf16[4,8,128,384]{2,3,1,0:T(8,128)(2,1)S(1)}, bf16[4,8,128,384]{2,3,1,0:T(8,128)(2,1)}, u32[]{:S(2)}) copy-start(bf16[4,8,128,384]{2,3,1,0:T(8,128)(2,1)} %get-tuple-element.384) | copy-start | bytes 9437188
  65.1 10.0 %all-to-all-start.1 = ((f32[8,1,16]{2,1,0:T(1,128)}), f32[8,1,16]{2,1,0:T(1,128)S(1)}, u32[]{:S(2)}, u32[]{:S(2)}) async-start(f32[8,1,16]{2,1,0:T(1,128)} %bitcast.32), calls=%async_computation.1 | async-start | bytes 8192 | tf_op jit(solution)/shard_map/all_to_all | solution.py:45
  69.6 75.7 %reduce-scatter.2.cloned.1.call-start = ((), (), s32[]{:S(2)}) async-start(), calls=%async_computation.3 | async-start | bytes 1310720 | tf_op jit(solution)/shard_map/reduce_scatter | solution.py:121
  79.6 2.0 %copy-start.3 = (bf16[4,128,8,128]{1,3,2,0:T(8,128)(2,1)}, bf16[4,128,8,128]{1,3,2,0:T(8,128)(2,1)S(1)}, u32[]{:S(2)}) copy-start(bf16[4,128,8,128]{1,3,2,0:T(8,128)(2,1)S(1)} %fusion.51) | copy-start | bytes 3145732
  86.4 2.9 %copy-start.6 = (bf16[4,128,8,128]{1,3,2,0:T(8,128)(2,1)S(1)}, bf16[4,128,8,128]{1,3,2,0:T(8,128)(2,1)}, u32[]{:S(2)}) copy-start(bf16[4,128,8,128]{1,3,2,0:T(8,128)(2,1)} %get-tuple-element.389) | copy-start | bytes 3145732 | tf_op jit(solution)/shard_map/while
  86.6 4.9 %copy-start.2 = (bf16[4,8,128,384]{2,3,1,0:T(8,128)(2,1)S(1)}, bf16[4,8,128,384]{2,3,1,0:T(8,128)(2,1)}, u32[]{:S(2)}) copy-start(bf16[4,8,128,384]{2,3,1,0:T(8,128)(2,1)} %get-tuple-element.413) | copy-start | bytes 9437188 | tf_op jit(solution)/shard_map/while
  90.6 1.0 copy-start.7
  94.0 3.0 %copy-start.6 = (bf16[4,128,8,128]{1,3,2,0:T(8,128)(2,1)S(1)}, bf16[4,128,8,128]{1,3,2,0:T(8,128)(2,1)}, u32[]{:S(2)}) copy-start(bf16[4,128,8,128]{1,3,2,0:T(8,128)(2,1)} %get-tuple-element.389) | copy-start | bytes 3145732 | tf_op jit(solution)/shard_map/while
  94.2 5.0 %copy-start.2 = (bf16[4,8,128,384]{2,3,1,0:T(8,128)(2,1)S(1)}, bf16[4,8,128,384]{2,3,1,0:T(8,128)(2,1)}, u32[]{:S(2)}) copy-start(bf16[4,8,128,384]{2,3,1,0:T(8,128)(2,1)} %get-tuple-element.413) | copy-start | bytes 9437188 | tf_op jit(solution)/shard_map/while
  98.2 1.0 copy-start.7
  101.6 3.0 %copy-start.6 = (bf16[4,128,8,128]{1,3,2,0:T(8,128)(2,1)S(1)}, bf16[4,128,8,128]{1,3,2,0:T(8,128)(2,1)}, u32[]{:S(2)}) copy-start(bf16[4,128,8,128]{1,3,2,0:T(8,128)(2,1)} %get-tuple-element.389) | copy-start | bytes 3145732 | tf_op jit(solution)/shard_map/while
  101.8 4.9 %copy-start.2 = (bf16[4,8,128,384]{2,3,1,0:T(8,128)(2,1)S(1)}, bf16[4,8,128,384]{2,3,1,0:T(8,128)(2,1)}, u32[]{:S(2)}) copy-start(bf16[4,8,128,384]{2,3,1,0:T(8,128)(2,1)} %get-tuple-element.413) | copy-start | bytes 9437188 | tf_op jit(solution)/shard_map/while
  105.8 1.0 copy-start.7
  109.2 3.0 %copy-start.6 = (bf16[4,128,8,128]{1,3,2,0:T(8,128)(2,1)S(1)}, bf16[4,128,8,128]{1,3,2,0:T(8,128)(2,1)}, u32[]{:S(2)}) copy-start(bf16[4,128,8,128]{1,3,2,0:T(8,128)(2,1)} %get-tuple-element.389) | copy-start | bytes 3145732 | tf_op jit(solution)/shard_map/while
  109.5 4.9 %copy-start.2 = (bf16[4,8,128,384]{2,3,1,0:T(8,128)(2,1)S(1)}, bf16[4,8,128,384]{2,3,1,0:T(8,128)(2,1)}, u32[]{:S(2)}) copy-start(bf16[4,8,128,384]{2,3,1,0:T(8,128)(2,1)} %get-tuple-element.413) | copy-start | bytes 9437188 | tf_op jit(solution)/shard_map/while
  113.4 1.0 copy-start.7
  117.6 1.1 copy-start.9
  119.0 1.6 %copy-start.8 = (bf16[4,128,8,128]{1,3,2,0:T(8,128)(2,1)S(1)}, bf16[4,128,8,128]{1,3,2,0:T(8,128)(2,1)}, u32[]{:S(2)}) copy-start(bf16[4,128,8,128]{1,3,2,0:T(8,128)(2,1)} %get-tuple-element.406) | copy-start | bytes 3145732
  (2 other events, 1.0 us)
Sparse Core Ops, SparseCore 0:
  120.3 24.9 reduce-scatter.1
where the time goes:
time: 155 us; the launch traced here: 154 us
  local copies, waits for them, and re-layouts  35.4 us (23%)
  matrix products  30.5 us (20%)
  waiting for transfers between devices  26.3 us (17%)
  other arithmetic  22.7 us (15%)
  between operations  16.2 us (10%)
  blocking collectives  11.5 us (7%)
  starting transfers between devices  10.8 us (7%)
    reduce_scatter x1, waiting for transfers between devices, body(): lax.psum_scatter(kv_grad[:prefix_rows], 'resp', scatter_dimension=0, tile...  22.6 us
    all_gather x1, blocking collectives, body(): prefix_all = lax.all_gather(prefix_kv[0], 'resp', axis=0, tiled=True)  11.5 us
    dot_general x4, matrix products, head_backward(): jnp.einsum('rgd,ld->grl', grad_head, value_head, preferred_element_type=j...  10.9 us
    unnamed x26, local copies, waits for them, and re-layouts  7.72 us
    dot_general x4, matrix products, head_forward(): jnp.einsum('grl,ld->rgd', prob_bf16, value_head, preferred_element_type=j...  6.96 us
    all_to_all x1, starting transfers between devices, body(): lax.all_to_all(sent_slot, 'dp', split_axis=0, concat_axis=0, tiled=True)  6.33 us
    dynamic_slice x8, local copies, waits for them, and re-layouts, body(): lax.map(head_backward, (key_heads, value_heads, prob_all, out_all, grad_h...  5.12 us
    while x40, local copies, waits for them, and re-layouts  4.94 us
  transfers between devices with their start and end apart: 3, of which 2 were waited for; matrix products, arithmetic and copies ran while one was open for 22% of the time, Pallas kernels for 0%

commit v1 on v0

--- a/solution.py
+++ b/solution.py
@@ -12,6 +12,12 @@
 loss_scale = 65536.0
 clip_lower = 0.8
 clip_upper = 1.28
+
+
+def laid_out(blocks, dim):
+    blocks = jnp.moveaxis(blocks, 0, dim)
+    shape = blocks.shape
+    return blocks.reshape(*shape[:dim], shape[dim] * shape[dim + 1], *shape[dim + 2 :])
 
 
 def split_heads(keys_values):
@@ -48,7 +54,14 @@
     old_rows = (
         jnp.zeros((tok_rows,), jnp.float32).at[got_slot.reshape(-1)].set(got_logprob.reshape(-1))
     )
-    prefix_all = lax.all_gather(prefix_kv[0], "resp", axis=0, tiled=True)
+    size = lax.axis_size("resp")
+    forward = [(i, (i + 1) % size) for i in range(size)]
+    parts = [prefix_kv[0]]
+    while len(parts) < size:
+        parts.append(lax.ppermute(parts[-1], "resp", forward))
+    index = lax.axis_index("resp")
+    parts = jnp.stack(parts)[(index - jnp.arange(size)) % size]
+    prefix_all = laid_out(parts, 0)
     prefix_rows = prefix_all.shape[0]
     total_keys = prefix_rows + tok_rows
     own_kv = resp_kv[0, 0]

time: 155 us -> 145 us (0.935)
  blocking collectives: 11.5 us -> 0 us
  local copies, waits for them, and re-layouts: 35.4 us -> 30.1 us
  starting transfers between devices: 10.8 us -> 15.9 us
  waiting for transfers between devices: 26.3 us -> 28.8 us
    all_gather x1 -> x0, blocking collectives: 11.5 us -> none  [body(): prefix_all = lax.all_gather(prefix_kv[0], 'resp', axis=0, tiled=True)]
    ppermute x0 -> x3, starting transfers between devices: none -> 6.03 us  [body(): parts.append(lax.ppermute(parts[-1], 'resp', forward))]
    dynamic_slice x8, local copies, waits for them, and re-layouts: 4.6 us -> 0.8 us  [body(): lax.map(head_forward, (query_heads, key_heads, value_heads))]
    ppermute x0 -> x3, waiting for transfers between devices: none -> 3.36 us  [body(): parts.append(lax.ppermute(parts[-1], 'resp', forward))]
    all_to_all x1, waiting for transfers between devices: 3.66 us -> 0.86 us  [body(): lax.all_to_all(sent_logprob, 'dp', split_axis=0, concat_axis=0, tiled=True)]
    reduce_scatter x1, waiting for transfers between devices: 22.6 us -> 24.4 us  [body(): lax.psum_scatter(kv_grad[:prefix_rows], 'resp', scatter_dimension=0, tile...]
    unnamed x26 -> x27, local copies, waits for them, and re-layouts: 7.72 us -> 6.2 us
    while x40 -> x16, local copies, waits for them, and re-layouts: 4.94 us -> 3.88 us
  transfers between devices with their start and end apart: 3 -> 6, of which waited for: 2 -> 4; matrix products, arithmetic and copies ran while one was open for 22% -> 10% of each run, Pallas kernels for 0% -> 0%
where the time goes in v1:
time: 145 us; the launch traced here: 144 us
  local copies, waits for them, and re-layouts  30.1 us (21%)
  matrix products  30 us (21%)
  waiting for transfers between devices  28.8 us (20%)
  other arithmetic  22.4 us (15%)
  between operations  16.3 us (11%)
  starting transfers between devices  15.9 us (11%)
    reduce_scatter x1, waiting for transfers between devices, body(): lax.psum_scatter(kv_grad[:prefix_rows], 'resp', scatter_dimension=0, tile...  24.4 us
    dot_general x4, matrix products, head_backward(): jnp.einsum('rgd,ld->grl', grad_head, value_head, preferred_element_type=j...  10.5 us
    dot_general x4, matrix products, head_forward(): jnp.einsum('grl,ld->rgd', prob_bf16, value_head, preferred_element_type=j...  6.96 us
    unnamed x27, local copies, waits for them, and re-layouts  6.2 us
    ppermute x3, starting transfers between devices, body(): parts.append(lax.ppermute(parts[-1], 'resp', forward))  6.03 us
    dynamic_slice x8, local copies, waits for them, and re-layouts, body(): lax.map(head_backward, (key_heads, value_heads, prob_all, out_all, grad_h...  5.12 us
    all_to_all x1, starting transfers between devices, body(): lax.all_to_all(sent_logprob, 'dp', split_axis=0, concat_axis=0, tiled=True)  4.94 us
    dot_general x4, matrix products, head_backward(): jnp.einsum('grl,ld->rgd', dscore, key_head, preferred_element_type=jnp.fl...  4.9 us
  transfers between devices with their start and end apart: 6, of which 4 were waited for; matrix products, arithmetic and copies ran while one was open for 10% of the time, Pallas kernels for 0%

profile of v1, /device:TPU:0, one launch (start us, length us, event | category | flops | bytes accessed | tf_op | source)
XLA Modules:
  0.0 143.7 jit_solution(7376227486751670648)
XLA Ops:
  7.2 3.0 %collective-permute-start = (bf16[64,1024]{1,0:T(8,128)(2,1)}, bf16[64,1024]{1,0:T(8,128)(2,1)S(1)}, u32[]{:S(2)}, u32[]{:S(2)}) collective-permute-start(bf16[64,1024]{1,0:T(8,128)(2,1)} %bitcast.242), channel_id=1, source_target_pairs={{0,1},{1,2},{2,3},{3,0},{4,5},{5,6},{6,7},{7,4},{8,9},{9,10},{10,1... | collective-permute-start | bytes 393224 | tf_op jit(solution)/shard_map/ppermute | solution.py:61
  10.8 2.5 %sort.17 = (s32[128]{0:T(128)}, s32[128]{0:T(128)S(1)}) sort(s32[128]{0:T(128)S(1)} %get-tuple-element.212, s32[128]{0:T(128)S(1)} %iota.34), dimensions={0}, to_apply=%region_4.5 | sort | flops 896 | bytes 2048 | tf_op jit(solution)/shard_map/jit(argsort)/sort | solution.py:47
  13.4 1.2 gather_fusion.1
  15.3 4.9 %all-to-all-start = ((s32[8,1,16]{2,1,0:T(1,128)}), s32[8,1,16]{2,1,0:T(1,128)S(1)}, u32[]{:S(2)}, u32[]{:S(2)}) async-start(s32[8,1,16]{2,1,0:T(1,128)} %bitcast.34), calls=%async_computation | async-start | bytes 8192 | tf_op jit(solution)/shard_map/all_to_all | solution.py:52
  21.4 1.5 %collective-permute-start.1 = (bf16[64,1024]{1,0:T(8,128)(2,1)S(1)}, bf16[64,1024]{1,0:T(8,128)(2,1)}, u32[]{:S(2)}, u32[]{:S(2)}) collective-permute-start(bf16[64,1024]{1,0:T(8,128)(2,1)S(1)} %collective-permute-done), channel_id=1, source_target_pairs={{0,1},{1,2},{2,3},{3,0},{4,5},{5,6},{6,7},{7,4},{8,9},{9,10},{10,1... | collective-permute-start | bytes 393224 | tf_op jit(solution)/shard_map/ppermute | solution.py:61
  23.6 1.2 gather_fusion.2
  25.7 4.9 %all-to-all-start.1 = ((f32[8,1,16]{2,1,0:T(1,128)}), f32[8,1,16]{2,1,0:T(1,128)S(1)}, u32[]{:S(2)}, u32[]{:S(2)}) async-start(f32[8,1,16]{2,1,0:T(1,128)} %bitcast.37), calls=%async_computation.1 | async-start | bytes 8192 | tf_op jit(solution)/shard_map/all_to_all | solution.py:51
  32.7 1.3 copy.68
  37.4 1.5 %collective-permute-start.2 = (bf16[64,1024]{1,0:T(8,128)(2,1)}, bf16[64,1024]{1,0:T(8,128)(2,1)S(1)}, u32[]{:S(2)}, u32[]{:S(2)}) collective-permute-start(bf16[64,1024]{1,0:T(8,128)(2,1)} %collective-permute-done.1), channel_id=1, source_target_pairs={{0,1},{1,2},{2,3},{3,0},{4,5},{5,6},{6,7},{7,4},{8,9},{9,10},{10,1... | collective-permute-start | bytes 393224 | tf_op jit(solution)/shard_map/ppermute | solution.py:61
  38.9 1.5 %scatter_custom_fusion = f32[128]{0:T(128)} fusion(s32[128]{0:T(128)S(1)} %fusion.63, f32[128]{0:T(128)S(1)} %reshape.210, f32[]{:T(128)} %constant.105.clone.1), kind=kCustom, calls=%fused_computation.98 | custom fusion | bytes 516 | tf_op jit(solution)/shard_map/scatter | solution.py:55
  40.4 3.4 %collective-permute-done.2 = bf16[64,1024]{1,0:T(8,128)(2,1)S(1)} collective-permute-done((bf16[64,1024]{1,0:T(8,128)(2,1)}, bf16[64,1024]{1,0:T(8,128)(2,1)S(1)}, u32[]{:S(2)}, u32[]{:S(2)}) %collective-permute-start.2) | collective-permute-done | bytes 131104 | tf_op jit(solution)/shard_map/ppermute | solution.py:61
  45.8 2.4 %broadcast.166.clone = bf16[4,8,128,384]{2,3,1,0:T(8,128)(2,1)} broadcast(bf16[]{:T(256)} %constant.106.clone.1), dimensions={} | broadcast | bytes 3145730 | tf_op jit(solution)/shard_map/broadcast.16
  48.2 14.7 %while.28 = (s32[]{:T(128)}, bf16[4,8,128,384]{2,3,1,0:T(8,128)(2,1)}, f32[4,128,8,128]{1,3,2,0:T(8,128)}, bf16[4,384,128]{1,2,0:T(8,128)(2,1)S(1)}, bf16[4,128,...) while((s32[]{:T(128)}, ...), condition=%wide.region_3.4_spmd.clone.clone, body=%wide.region_0.0_spmd.clone.sunk.clone | while | flops 306464512 | bytes 5441373 | solution.py:92
  50.1 1.7 %fusion.115 = f32[4,128,8,128]{1,3,2,0:T(8,128)} fusion(f32[4,128,8,128]{1,3,2,0:T(8,128)} %get-tuple-element.381, s32[]{:T(128)} %get-tuple-element.379, bf16[4,384,128]{1,2,0:T(8,128)(2,1)S(1)} %get-tuple-element.393, f32[8,128]{1,0:T(8,128)S(1)} %get-tuple-element.359, pred[128,384]{0,1:T(8,128)(4,1)S(1)} %fusion.113, ...), kind=kOutput, calls=%fused_computation.29.clone.1.clone | convolution fusion | flops 203294080 | bytes 1038336 | tf_op jit(solution)/shard_map/while/body/eval_jaxpr/grl,ld->rgd/dot_general | solution.py:87
  53.8 1.8 %fusion.115 = f32[4,128,8,128]{1,3,2,0:T(8,128)} fusion(f32[4,128,8,128]{1,3,2,0:T(8,128)} %get-tuple-element.381, s32[]{:T(128)} %get-tuple-element.379, bf16[4,384,128]{1,2,0:T(8,128)(2,1)S(1)} %get-tuple-element.393, f32[8,128]{1,0:T(8,128)S(1)} %get-tuple-element.359, pred[128,384]{0,1:T(8,128)(4,1)S(1)} %fusion.113, ...), kind=kOutput, calls=%fused_computation.29.clone.1.clone | convolution fusion | flops 203294080 | bytes 1038336 | tf_op jit(solution)/shard_map/while/body/eval_jaxpr/grl,ld->rgd/dot_general | solution.py:87
  57.5 1.7 %fusion.115 = f32[4,128,8,128]{1,3,2,0:T(8,128)} fusion(f32[4,128,8,128]{1,3,2,0:T(8,128)} %get-tuple-element.381, s32[]{:T(128)} %get-tuple-element.379, bf16[4,384,128]{1,2,0:T(8,128)(2,1)S(1)} %get-tuple-element.393, f32[8,128]{1,0:T(8,128)S(1)} %get-tuple-element.359, pred[128,384]{0,1:T(8,128)(4,1)S(1)} %fusion.113, ...), kind=kOutput, calls=%fused_computation.29.clone.1.clone | convolution fusion | flops 203294080 | bytes 1038336 | tf_op jit(solution)/shard_map/while/body/eval_jaxpr/grl,ld->rgd/dot_general | solution.py:87
  61.1 1.7 %fusion.115 = f32[4,128,8,128]{1,3,2,0:T(8,128)} fusion(f32[4,128,8,128]{1,3,2,0:T(8,128)} %get-tuple-element.381, s32[]{:T(128)} %get-tuple-element.379, bf16[4,384,128]{1,2,0:T(8,128)(2,1)S(1)} %get-tuple-element.393, f32[8,128]{1,0:T(8,128)S(1)} %get-tuple-element.359, pred[128,384]{0,1:T(8,128)(4,1)S(1)} %fusion.113, ...), kind=kOutput, calls=%fused_computation.29.clone.1.clone | convolution fusion | flops 203294080 | bytes 1038336 | tf_op jit(solution)/shard_map/while/body/eval_jaxpr/grl,ld->rgd/dot_general | solution.py:87
  63.8 3.1 %bitcast_convert_fusion = f32[128,4096]{0,1:T(8,128)} fusion(f32[4,128,8,128]{1,3,2,0:T(8,128)} %get-tuple-element.404), kind=kLoop, calls=%fused_computation.55 | loop fusion | flops 1048576 | bytes 4194304
  66.9 1.9 %copy.82 = f32[128,4096]{1,0:T(8,128)S(1)} copy(f32[128,4096]{0,1:T(8,128)} %bitcast_convert_fusion) | data formatting | bytes 4194304
  68.8 1.7 %multiply_reduce_fusion = f32[128]{0:T(128)S(1)} fusion(f32[128,4096]{1,0:T(8,128)S(1)} %copy.82, bf16[1,1,128,4096]{3,2,1,0:T(8,128)(2,1)} %param.17), kind=kLoop, calls=%fused_computation.50 | loop fusion | flops 1572736 | bytes 3146240 | tf_op jit(solution)/shard_map/rj,rj->r/dot_general | solution.py:96
  70.6 1.5 %fusion.51 = bf16[4,128,8,128]{1,3,2,0:T(8,128)(2,1)S(1)} fusion(bf16[128,4,8,128]{0,3,2,1:T(8,128)(2,1)} %bitcast.234, f32[128]{0:T(128)S(1)} %compare_select_fusion.5), kind=kLoop, calls=%fused_computation.53 | loop fusion | flops 1572864 | bytes 2097664 | tf_op jit(solution)/shard_map/transpose | solution.py:107
  72.1 2.0 %fusion.74 = f32[4,128,384,1]{2,1,3,0:T(8,128)} fusion(bf16[4,128,8,128]{1,3,2,0:T(8,128)(2,1)S(1)} %fusion.51, bf16[4,8,128,384]{2,3,1,0:T(8,128)(2,1)S(1)} %copy-done.1), kind=kOutput, calls=%fused_computation.103 | convolution fusion | flops 402653184 | bytes 4980736 | tf_op jit(solution)/shard_map/hgrl,hrgd->lhd/dot_general | solution.py:128
  74.1 2.4 %broadcast.166 = bf16[4,8,128,384]{2,3,1,0:T(8,128)(2,1)} broadcast(bf16[]{:T(256)} %constant.106.clone.1), dimensions={} | broadcast | bytes 3145730 | tf_op jit(solution)/shard_map/broadcast.16
  76.5 26.3 %while.27 = (s32[]{:T(128)}, bf16[4,128,8,128]{1,3,2,0:T(8,128)(2,1)}, bf16[4,8,128,384]{2,3,1,0:T(8,128)(2,1)}, bf16[4,384,128]{1,2,0:T(8,128)(2,1)}, bf16[4,8,...) while((s32[]{:T(128)}, ...), condition=%wide.region_8.9_spmd.clone, body=%wide.region_6.8_spmd.sunk.clone | while | flops 203684864 | bytes 16460437 | solution.py:121
  78.3 2.6 %bitcast_dynamic-update-slice_fusion.6 = (bf16[4,8,128,384]{2,3,1,0:T(8,128)(2,1)}, bf16[8,128,384]{1,2,0:T(8,128)(2,1)S(1)}) fusion(bf16[4,8,128,384]{2,3,1,0:T(8,128)(2,1)} %get-tuple-element.407, s32[]{:T(128)} %get-tuple-element.405, f32[8,128]{1,0:T(8,128)S(1)} %bitcast.240, bf16[4,128,8,128]{1,3,2,0:T(8,128)(2,1)S(1)} %get-tuple-element.419, ...), kind=kOutput, calls=%fused_computation.11.clone.1.clone | convolution fusion | flops 102629376 | bytes 2725376 | tf_op jit(solution)/shard_map/while/body/eval_jaxpr/rgd,ld->grl/dot_general | solution.py:111
  84.8 2.6 %bitcast_dynamic-update-slice_fusion.6 = (bf16[4,8,128,384]{2,3,1,0:T(8,128)(2,1)}, bf16[8,128,384]{1,2,0:T(8,128)(2,1)S(1)}) fusion(bf16[4,8,128,384]{2,3,1,0:T(8,128)(2,1)} %get-tuple-element.407, s32[]{:T(128)} %get-tuple-element.405, f32[8,128]{1,0:T(8,128)S(1)} %bitcast.240, bf16[4,128,8,128]{1,3,2,0:T(8,128)(2,1)S(1)} %get-tuple-element.419, ...), kind=kOutput, calls=%fused_computation.11.clone.1.clone | convolution fusion | flops 102629376 | bytes 2725376 | tf_op jit(solution)/shard_map/while/body/eval_jaxpr/rgd,ld->grl/dot_general | solution.py:111
  91.4 2.6 %bitcast_dynamic-update-slice_fusion.6 = (bf16[4,8,128,384]{2,3,1,0:T(8,128)(2,1)}, bf16[8,128,384]{1,2,0:T(8,128)(2,1)S(1)}) fusion(bf16[4,8,128,384]{2,3,1,0:T(8,128)(2,1)} %get-tuple-element.407, s32[]{:T(128)} %get-tuple-element.405, f32[8,128]{1,0:T(8,128)S(1)} %bitcast.240, bf16[4,128,8,128]{1,3,2,0:T(8,128)(2,1)S(1)} %get-tuple-element.419, ...), kind=kOutput, calls=%fused_computation.11.clone.1.clone | convolution fusion | flops 102629376 | bytes 2725376 | tf_op jit(solution)/shard_map/while/body/eval_jaxpr/rgd,ld->grl/dot_general | solution.py:111
  97.9 2.7 %bitcast_dynamic-update-slice_fusion.6 = (bf16[4,8,128,384]{2,3,1,0:T(8,128)(2,1)}, bf16[8,128,384]{1,2,0:T(8,128)(2,1)S(1)}) fusion(bf16[4,8,128,384]{2,3,1,0:T(8,128)(2,1)} %get-tuple-element.407, s32[]{:T(128)} %get-tuple-element.405, f32[8,128]{1,0:T(8,128)S(1)} %bitcast.240, bf16[4,128,8,128]{1,3,2,0:T(8,128)(2,1)S(1)} %get-tuple-element.419, ...), kind=kOutput, calls=%fused_computation.11.clone.1.clone | convolution fusion | flops 102629376 | bytes 2725376 | tf_op jit(solution)/shard_map/while/body/eval_jaxpr/rgd,ld->grl/dot_general | solution.py:111
  102.8 2.9 %fusion.73 = f32[4,384,128,1]{1,2,3,0:T(8,128)S(1)} fusion(bf16[4,8,128,384]{2,3,1,0:T(8,128)(2,1)} %get-tuple-element.89, bf16[4,128,8,128]{1,3,2,0:T(8,128)(2,1)S(1)} %get-tuple-element.422), kind=kOutput, calls=%fused_computation.102 | convolution fusion | flops 402653184 | bytes 4980736 | tf_op jit(solution)/shard_map/hgrl,hrgd->lhd/dot_general | solution.py:125
  108.8 1.3 copy.88
  110.8 24.4 %reduce-scatter.2.cloned.1.call-done = f32[64,1024]{1,0:T(8,128)} async-done(((f32[256,1024]{1,0:T(8,128)}), f32[64,1024]{1,0:T(8,128)}) %reduce-scatter.2.cloned.1.call-update) | async-done | bytes 262160 | tf_op jit(solution)/shard_map/reduce_scatter | solution.py:134
  135.2 1.6 %convert_bitcast_fusion = bf16[1,64,1024]{2,1,0:T(8,128)(2,1)} fusion(f32[64,1024]{1,0:T(8,128)} %reduce-scatter.2.cloned.1.call-done), kind=kLoop, calls=%fused_computation.64 | loop fusion | flops 65536 | bytes 393216 | tf_op jit(solution)/shard_map/broadcast_in_dim | solution.py:139
  (112 shorter events, 37.4 us)
Async XLA Ops:
  7.2 16.4 %copy-start = (f32[1,1,128]{2,1,0:T(1,128)S(1)}, f32[1,1,128]{2,1,0:T(1,128)}, u32[]{:S(2)}) copy-start(f32[1,1,128]{2,1,0:T(1,128)} %param.19) | copy-start | bytes 1540
  7.2 23.5 %copy-start.9 = (bf16[1,1,128,4096]{3,2,1,0:T(8,128)(2,1)S(1)}, bf16[1,1,128,4096]{3,2,1,0:T(8,128)(2,1)}, u32[]{:S(2)}) copy-start(bf16[1,1,128,4096]{3,2,1,0:T(8,128)(2,1)} %param.14) | copy-start | bytes 3145732
  7.2 14.2 %collective-permute-start = (bf16[64,1024]{1,0:T(8,128)(2,1)}, bf16[64,1024]{1,0:T(8,128)(2,1)S(1)}, u32[]{:S(2)}, u32[]{:S(2)}) collective-permute-start(bf16[64,1024]{1,0:T(8,128)(2,1)} %bitcast.242), channel_id=1, source_target_pairs={{0,1},{1,2},{2,3},{3,0},{4,5},{5,6},{6,7},{7,4},{8,9},{9,10},{10,1... | collective-permute-start | bytes 393224 | tf_op jit(solution)/shard_map/ppermute | solution.py:61
  13.4 19.3 %copy-start.2 = (bf16[1,1,128,4096]{3,2,1,0:T(8,128)(2,1)S(1)}, bf16[1,1,128,4096]{3,2,1,0:T(8,128)(2,1)}, u32[]{:S(2)}) copy-start(bf16[1,1,128,4096]{3,2,1,0:T(8,128)(2,1)} %param.17) | copy-start | bytes 3145732
  15.3 10.4 %all-to-all-start = ((s32[8,1,16]{2,1,0:T(1,128)}), s32[8,1,16]{2,1,0:T(1,128)S(1)}, u32[]{:S(2)}, u32[]{:S(2)}) async-start(s32[8,1,16]{2,1,0:T(1,128)} %bitcast.34), calls=%async_computation | async-start | bytes 8192 | tf_op jit(solution)/shard_map/all_to_all | solution.py:52
  21.4 15.9 %collective-permute-start.1 = (bf16[64,1024]{1,0:T(8,128)(2,1)S(1)}, bf16[64,1024]{1,0:T(8,128)(2,1)}, u32[]{:S(2)}, u32[]{:S(2)}) collective-permute-start(bf16[64,1024]{1,0:T(8,128)(2,1)S(1)} %collective-permute-done), channel_id=1, source_target_pairs={{0,1},{1,2},{2,3},{3,0},{4,5},{5,6},{6,7},{7,4},{8,9},{9,10},{10,1... | collective-permute-start | bytes 393224 | tf_op jit(solution)/shard_map/ppermute | solution.py:61
  25.7 10.4 %all-to-all-start.1 = ((f32[8,1,16]{2,1,0:T(1,128)}), f32[8,1,16]{2,1,0:T(1,128)S(1)}, u32[]{:S(2)}, u32[]{:S(2)}) async-start(f32[8,1,16]{2,1,0:T(1,128)} %bitcast.37), calls=%async_computation.1 | async-start | bytes 8192 | tf_op jit(solution)/shard_map/all_to_all | solution.py:51
  30.6 104.6 %reduce-scatter.2.cloned.1.call-start = ((), (), s32[]{:S(2)}) async-start(), calls=%async_computation.3 | async-start | bytes 1310720 | tf_op jit(solution)/shard_map/reduce_scatter | solution.py:134
  30.7 13.1 %copy-start.11 = (bf16[1,64,1024]{2,1,0:T(8,128)(2,1)S(1)}, bf16[1,64,1024]{2,1,0:T(8,128)(2,1)}, u32[]{:S(2)}) copy-start(bf16[1,64,1024]{2,1,0:T(8,128)(2,1)} %param.15) | copy-start | bytes 393220
  32.7 12.6 %copy-start.10 = (bf16[1,1,128,1024]{3,2,1,0:T(8,128)(2,1)S(1)}, bf16[1,1,128,1024]{3,2,1,0:T(8,128)(2,1)}, u32[]{:S(2)}) copy-start(bf16[1,1,128,1024]{3,2,1,0:T(8,128)(2,1)} %param.16) | copy-start | bytes 786436
  37.4 6.4 %collective-permute-start.2 = (bf16[64,1024]{1,0:T(8,128)(2,1)}, bf16[64,1024]{1,0:T(8,128)(2,1)S(1)}, u32[]{:S(2)}, u32[]{:S(2)}) collective-permute-start(bf16[64,1024]{1,0:T(8,128)(2,1)} %collective-permute-done.1), channel_id=1, source_target_pairs={{0,1},{1,2},{2,3},{3,0},{4,5},{5,6},{6,7},{7,4},{8,9},{9,10},{10,1... | collective-permute-start | bytes 393224 | tf_op jit(solution)/shard_map/ppermute | solution.py:61
  62.9 0.8 copy-start.7
  62.9 0.9 copy-start.8
  68.8 1.7 %copy-start.12 = (f32[1,1,128]{2,1,0:T(1,128)S(1)}, f32[1,1,128]{2,1,0:T(1,128)}, u32[]{:S(2)}) copy-start(f32[1,1,128]{2,1,0:T(1,128)} %param.18) | copy-start | bytes 1540
  68.8 1.7 %copy-start.13 = (f32[128]{0:T(128)S(1)}, f32[128]{0:T(128)}, u32[]{:S(2)}) copy-start(f32[128]{0:T(128)} %scatter_custom_fusion) | copy-start | bytes 1540
  68.8 3.3 %copy-start.1 = (bf16[4,8,128,384]{2,3,1,0:T(8,128)(2,1)S(1)}, bf16[4,8,128,384]{2,3,1,0:T(8,128)(2,1)}, u32[]{:S(2)}) copy-start(bf16[4,8,128,384]{2,3,1,0:T(8,128)(2,1)} %get-tuple-element.401) | copy-start | bytes 9437188
  78.0 2.8 %copy-start.3 = (bf16[4,128,8,128]{1,3,2,0:T(8,128)(2,1)S(1)}, bf16[4,128,8,128]{1,3,2,0:T(8,128)(2,1)}, u32[]{:S(2)}) copy-start(bf16[4,128,8,128]{1,3,2,0:T(8,128)(2,1)} %get-tuple-element.406) | copy-start | bytes 3145732 | tf_op jit(solution)/shard_map/while
  82.1 1.0 copy-start.4
  84.6 2.8 %copy-start.3 = (bf16[4,128,8,128]{1,3,2,0:T(8,128)(2,1)S(1)}, bf16[4,128,8,128]{1,3,2,0:T(8,128)(2,1)}, u32[]{:S(2)}) copy-start(bf16[4,128,8,128]{1,3,2,0:T(8,128)(2,1)} %get-tuple-element.406) | copy-start | bytes 3145732 | tf_op jit(solution)/shard_map/while
  88.7 1.0 copy-start.4
  91.1 2.9 %copy-start.3 = (bf16[4,128,8,128]{1,3,2,0:T(8,128)(2,1)S(1)}, bf16[4,128,8,128]{1,3,2,0:T(8,128)(2,1)}, u32[]{:S(2)}) copy-start(bf16[4,128,8,128]{1,3,2,0:T(8,128)(2,1)} %get-tuple-element.406) | copy-start | bytes 3145732 | tf_op jit(solution)/shard_map/while
  95.2 1.0 copy-start.4
  97.7 2.9 %copy-start.3 = (bf16[4,128,8,128]{1,3,2,0:T(8,128)(2,1)S(1)}, bf16[4,128,8,128]{1,3,2,0:T(8,128)(2,1)}, u32[]{:S(2)}) copy-start(bf16[4,128,8,128]{1,3,2,0:T(8,128)(2,1)} %get-tuple-element.406) | copy-start | bytes 3145732 | tf_op jit(solution)/shard_map/while
  101.8 1.0 copy-start.4
  105.8 1.1 copy-start.6
  107.2 1.6 %copy-start.5 = (bf16[4,128,8,128]{1,3,2,0:T(8,128)(2,1)S(1)}, bf16[4,128,8,128]{1,3,2,0:T(8,128)(2,1)}, u32[]{:S(2)}) copy-start(bf16[4,128,8,128]{1,3,2,0:T(8,128)(2,1)} %get-tuple-element.88) | copy-start | bytes 3145732
Sparse Core Ops, SparseCore 0:
  108.4 26.7 reduce-scatter.1
